TPU v7x, 256 devices: a whole 4x4x8 slice. The times are simulated.
256 devices in a mesh: row: 16 (over y_hi, z), col: 8 (over x, core), rhs: 2 (over y_lo).
Axes of the slice: x: 4, y: 4 (y_hi: 2, y_lo: 2; y = y_hi * 2 + y_lo), z: 8, core: 2. Of those that a mesh axis runs over, the one named last changes fastest.
Arguments:
- lower: float32 [6, 2048, 4, 2048], P(None, 'row', None, 'col'), may hold values from -0.0625 to 0.0625
- inverse: float32 [4, 2048, 2048], P(None, ('col', 'rhs'), 'row'), may hold values from -0.125 to 0.125
- right_side: float32 [6, 2048, 2048], P(None, 'row', 'rhs'), may hold values from -6 to 6
Outputs:
- solved: float32 [4, 2048, 2048], P(None, 'col', 'rhs')
- trailing: float32 [2, 2048, 2048], P(None, 'row', 'rhs')
All inputs are finite; a program needn't handle non-finite values.
Results may differ from a plain program's by a relative error of at most 0.0001.
Values sent between devices are 32-bit elements; how exact they have to be, the bound alone decides.
No kernel may reach another device: no remote copies, remote signals or barrier semaphores. Data moves between devices by JAX's collectives and lax.ppermute only.
A program may use at most 64 MiB of HBM per device.

v0:
```python
import jax
import jax.numpy as jnp
from jax import lax
from jax.sharding import PartitionSpec as P


def apply_block(lower, unknowns, k):
    return jnp.einsum(
        "inc,cr->inr", lower[k + 1 :, :, k, :], unknowns, precision=lax.Precision.HIGHEST
    )


def solve_block(inverse, residual_block, k):
    inverse_rows = lax.all_gather(inverse[k], "rhs", axis=0, tiled=True)
    partial_value = jnp.dot(
        inverse_rows,
        residual_block,
        precision=lax.Precision.HIGHEST,
        preferred_element_type=jnp.float32,
    )
    return lax.psum(partial_value, "row")


def on_device(lower, inverse, right_side):
    chain_len = inverse.shape[0]
    solved_list = []
    current = right_side
    for k in range(chain_len):
        unknowns = solve_block(inverse, current[k], k)
        solved_list.append(unknowns)
        summed = lax.psum(apply_block(lower, unknowns, k), "col")
        current = jnp.concatenate([current[: k + 1], current[k + 1 :] - summed], axis=0)
    trailing = current[chain_len:]
    return (jnp.stack(solved_list), trailing)


def solution(mesh):
    placed = (P(None, "row", None, "col"), P(None, ("col", "rhs"), "row"), P(None, "row", "rhs"))
    return jax.shard_map(
        on_device,
        mesh=mesh,
        in_specs=placed,
        out_specs=(P(None, "col", "rhs"), P(None, "row", "rhs")),
        check_vma=False,
    )
```

profile of v0, /device:TPU:8, one launch (start us, length us, event | category | flops | bytes accessed | tf_op | source)
XLA Modules:
  0.0 973.4 jit_solution(6360658621553922762)
XLA Ops:
  8.2 5.1 all-gather
  13.2 3.0 fusion.4
  16.3 2.2 slice.51
  18.5 158.9 %all-reduce.9.cloned.1.call-done = f32[256,1024]{1,0:T(8,128)} async-done(((f32[256,1024]{1,0:T(8,128)}), f32[256,1024]{1,0:T(8,128)}) %all-reduce.9.cloned.1.call-update) | async-done | bytes 1048592 | tf_op jit(solution)/shard_map/psum | solution.py:21
  177.4 7.8 convolution_bitcast_fusion
  185.3 1.7 slice-done
  187.0 2.1 copy.29
  189.1 4.9 all-gather.1
  194.0 62.1 %all-reduce.11.cloned.1.call-done = f32[5,128,1024]{1,2,0:T(8,128)} async-done(((f32[5,128,1024]{1,2,0:T(8,128)}), f32[5,128,1024]{1,2,0:T(8,128)}) %all-reduce.11.cloned.1.call-update) | async-done | bytes 2621456 | tf_op jit(solution)/shard_map/psum | solution.py:31
  256.1 2.8 sub.12
  258.9 2.0 convolution_bitcast_fusion.6
  261.1 2.1 slice.55
  263.3 155.9 %all-reduce.13.cloned.1.call-done = f32[256,1024]{1,0:T(8,128)} async-done(((f32[256,1024]{1,0:T(8,128)}), f32[256,1024]{1,0:T(8,128)}) %all-reduce.13.cloned.1.call-update) | async-done | bytes 1048592 | tf_op jit(solution)/shard_map/psum | solution.py:21
  419.1 6.0 convolution_bitcast_fusion.1
  425.2 4.9 all-gather.2
  430.1 64.3 %all-reduce.15.cloned.1.call-done = f32[4,128,1024]{1,2,0:T(8,128)} async-done(((f32[4,128,1024]{1,2,0:T(8,128)}), f32[4,128,1024]{1,2,0:T(8,128)}) %all-reduce.15.cloned.1.call-update) | async-done | bytes 2097168 | tf_op jit(solution)/shard_map/psum | solution.py:31
  494.4 1.8 slice_subtract_fusion
  496.2 1.3 copy-done
  497.5 2.0 convolution_bitcast_fusion.5
  499.6 2.0 slice.59
  501.5 156.2 %all-reduce.17.cloned.1.call-done = f32[256,1024]{1,0:T(8,128)} async-done(((f32[256,1024]{1,0:T(8,128)}), f32[256,1024]{1,0:T(8,128)}) %all-reduce.17.cloned.1.call-update) | async-done | bytes 1048592 | tf_op jit(solution)/shard_map/psum | solution.py:21
  657.7 5.8 convolution_bitcast_fusion.2
  663.6 4.9 all-gather.3
  668.6 62.6 %all-reduce.19.cloned.1.call-done = f32[3,128,1024]{1,2,0:T(8,128)} async-done(((f32[3,128,1024]{1,2,0:T(8,128)}), f32[3,128,1024]{1,2,0:T(8,128)}) %all-reduce.19.cloned.1.call-update) | async-done | bytes 1572880 | tf_op jit(solution)/shard_map/psum | solution.py:31
  731.2 1.6 slice_subtract_fusion.1
  733.9 2.0 convolution_bitcast_fusion.4
  736.2 1.5 slice.63
  737.7 156.1 %all-reduce.21.cloned.1.call-done = f32[256,1024]{1,0:T(8,128)} async-done(((f32[256,1024]{1,0:T(8,128)}), f32[256,1024]{1,0:T(8,128)}) %all-reduce.21.cloned.1.call-update) | async-done | bytes 1048592 | tf_op jit(solution)/shard_map/psum | solution.py:21
  893.8 4.0 convolution_bitcast_fusion.3
  897.9 4.5 pad_maximum_fusion
  902.4 61.6 %all-reduce.23.cloned.1.call-done = f32[2,128,1024]{1,2,0:T(8,128)} async-done(((f32[2,128,1024]{1,2,0:T(8,128)}), f32[2,128,1024]{1,2,0:T(8,128)}) %all-reduce.23.cloned.1.call-update) | async-done | bytes 1048592 | tf_op jit(solution)/shard_map/psum | solution.py:31
  963.9 1.3 slice_subtract_fusion.2
  (28 shorter events, 4.3 us)
Async XLA Ops:
  7.2 170.2 %all-reduce.9.cloned.1.call-start = ((), (), s32[]{:S(2)}) async-start(), calls=%async_computation | async-start | bytes 2097152 | tf_op jit(solution)/shard_map/psum | solution.py:21
  16.2 239.9 %all-reduce.11.cloned.1.call-start = ((), (), s32[]{:S(2)}) async-start(), calls=%async_computation.1 | async-start | bytes 5242880 | tf_op jit(solution)/shard_map/psum | solution.py:31
  185.2 1.7 slice-start
  185.2 233.9 %all-reduce.13.cloned.1.call-start = ((), (), s32[]{:S(2)}) async-start(), calls=%async_computation.2 | async-start | bytes 2097152 | tf_op jit(solution)/shard_map/psum | solution.py:21
  260.9 233.5 %all-reduce.15.cloned.1.call-start = ((), (), s32[]{:S(2)}) async-start(), calls=%async_computation.3 | async-start | bytes 4194304 | tf_op jit(solution)/shard_map/psum | solution.py:31
  425.1 232.6 %all-reduce.17.cloned.1.call-start = ((), (), s32[]{:S(2)}) async-start(), calls=%async_computation.4 | async-start | bytes 2097152 | tf_op jit(solution)/shard_map/psum | solution.py:21
  496.2 1.3 copy-start
  499.5 231.7 %copy-start.1 = (f32[4,128,1024]{1,2,0:T(8,128)S(1)}, f32[4,128,1024]{1,2,0:T(8,128)}, u32[]{:S(2)}) copy-start(f32[4,128,1024]{1,2,0:T(8,128)} %copy-done) | copy-start | bytes 6291460
  499.5 231.7 %all-reduce.19.cloned.1.call-start = ((), (), s32[]{:S(2)}) async-start(), calls=%async_computation.5 | async-start | bytes 3145728 | tf_op jit(solution)/shard_map/psum | solution.py:31
  663.6 230.2 %all-reduce.21.cloned.1.call-start = ((), (), s32[]{:S(2)}) async-start(), calls=%async_computation.6 | async-start | bytes 2097152 | tf_op jit(solution)/shard_map/psum | solution.py:21
  732.8 1.2 copy-start.2
  735.9 162.0 %copy-start.4 = (f32[256,1024]{1,0:T(8,128)S(1)}, f32[256,1024]{1,0:T(8,128)}, u32[]{:S(2)}) copy-start(f32[256,1024]{1,0:T(8,128)} %all-reduce.13.cloned.1.call-done) | copy-start | bytes 3145732
  735.9 228.0 %all-reduce.23.cloned.1.call-start = ((), (), s32[]{:S(2)}) async-start(), calls=%async_computation.7 | async-start | bytes 2097152 | tf_op jit(solution)/shard_map/psum | solution.py:31
  897.9 66.1 %copy-start.3 = (f32[3,128,1024]{1,2,0:T(8,128)S(1)}, f32[3,128,1024]{1,2,0:T(8,128)}, u32[]{:S(2)}) copy-start(f32[3,128,1024]{1,2,0:T(8,128)} %copy-done.2) | copy-start | bytes 4718596
Sparse Core Ops, SparseCore 0:
  16.4 161.0 all-reduce.8
  185.4 70.7 all-reduce.10
  261.0 158.0 all-reduce.12
  425.3 69.0 all-reduce.14
  499.6 158.0 all-reduce.16
  663.7 67.4 all-reduce.18
  736.0 157.7 all-reduce.20
  898.0 65.9 all-reduce.22
where the time goes:
time: 974 us; the launch traced here: 973 us
  waiting for transfers between devices  878 us (90%)
  matrix products  32.5 us (3%)
  blocking collectives  19.8 us (2%)
  local copies, waits for them, and re-layouts  16.3 us (2%)
  between operations  14.2 us (1%)
  other arithmetic  12 us (1%)
    psum x4, waiting for transfers between devices, solve_block(): return lax.psum(partial_value, 'row')  627 us
    psum x4, waiting for transfers between devices, on_device(): summed = lax.psum(apply_block(lower, unknowns, k), 'col')  251 us
    dot_general x4, matrix products, apply_block(): jnp.einsum('inc,cr->inr', lower[k + 1:, :, k, :], unknowns, precision=lax...  23.6 us
    all_gather x4, blocking collectives, solve_block(): inverse_rows = lax.all_gather(inverse[k], 'rhs', axis=0, tiled=True)  19.8 us
  transfers between devices with their start and end apart: 8, of which 8 were waited for; matrix products, arithmetic and copies ran while one was open for 1% of the time, Pallas kernels for 0%

commit v1 on v0

--- a/solution.py
+++ b/solution.py
@@ -28,7 +28,7 @@
     for k in range(chain_len):
         unknowns = solve_block(inverse, current[k], k)
         solved_list.append(unknowns)
-        summed = lax.psum(apply_block(lower, unknowns, k), "col")
+        summed = jnp.sum(lax.all_gather(apply_block(lower, unknowns, k), "col"), axis=0)
         current = jnp.concatenate([current[: k + 1], current[k + 1 :] - summed], axis=0)
     trailing = current[chain_len:]
     return (jnp.stack(solved_list), trailing)

time: 974 us -> 1060 us (1.088)
  waiting for transfers between devices: 878 us -> 916 us
  other arithmetic: 12 us -> 41 us
  local copies, waits for them, and re-layouts: 16.3 us -> 34 us
    all_gather x0 -> x4, waiting for transfers between devices: none -> 285 us  [on_device(): lax.all_gather(apply_block(lower, unknowns, k), 'col')]
    psum x4 -> x0, waiting for transfers between devices: 251 us -> none  [on_device(): summed = lax.psum(apply_block(lower, unknowns, k), 'col')]
    reduce_sum x0 -> x4, other arithmetic: none -> 29.5 us  [on_device(): jnp.sum(lax.all_gather(apply_block(lower, unknowns, k), 'col'), axis=0)]
where the time goes in v1:
time: 1060 us; the launch traced here: 1050 us
  waiting for transfers between devices  916 us (86%)
  other arithmetic  41 us (4%)
  local copies, waits for them, and re-layouts  34 us (3%)
  matrix products  28.9 us (3%)
  blocking collectives  19.8 us (2%)
  between operations  14.3 us (1%)
    psum x4, waiting for transfers between devices, solve_block(): return lax.psum(partial_value, 'row')  630 us
    all_gather x4, waiting for transfers between devices, on_device(): lax.all_gather(apply_block(lower, unknowns, k), 'col')  285 us
    reduce_sum x4, other arithmetic, on_device(): jnp.sum(lax.all_gather(apply_block(lower, unknowns, k), 'col'), axis=0)  29.5 us
  transfers between devices with their start and end apart: 8, of which 8 were waited for; matrix products, arithmetic and copies ran while one was open for 1% of the time, Pallas kernels for 0%

profile of v1, /device:TPU:8, one launch (start us, length us, event | category | flops | bytes accessed | tf_op | source)
XLA Modules:
  0.0 1054.8 jit_solution(18017311559789292729)
XLA Ops:
  8.2 5.1 all-gather
  13.2 3.0 fusion.4
  16.3 2.2 slice.51
  18.5 158.9 %all-reduce.5.cloned.1.call-done = f32[256,1024]{1,0:T(8,128)} async-done(((f32[256,1024]{1,0:T(8,128)}), f32[256,1024]{1,0:T(8,128)}) %all-reduce.5.cloned.1.call-update) | async-done | bytes 1048592 | tf_op jit(solution)/shard_map/psum | solution.py:21
  177.4 6.3 convolution_bitcast_fusion
  183.7 2.1 copy.19
  187.6 2.1 copy.53
  189.7 4.9 all-gather.2
  194.6 94.7 %all-gather.13.cloned.1.call-done = f32[40,128,1024]{2,1,0:T(8,128)} async-done(((f32[5,128,1024]{2,1,0:T(8,128)}), f32[40,128,1024]{2,1,0:T(8,128)}) %all-gather.13.cloned.1.call-update) | async-done | bytes 20971536 | tf_op jit(solution)/shard_map/all_gather | solution.py:31
  289.3 8.4 reduce_sum.36
  297.7 2.1 copy.48
  299.8 2.8 sub.12
  302.6 2.0 convolution_bitcast_fusion.6
  304.8 2.1 slice.55
  307.0 157.0 %all-reduce.7.cloned.1.call-done = f32[256,1024]{1,0:T(8,128)} async-done(((f32[256,1024]{1,0:T(8,128)}), f32[256,1024]{1,0:T(8,128)}) %all-reduce.7.cloned.1.call-update) | async-done | bytes 1048592 | tf_op jit(solution)/shard_map/psum | solution.py:21
  464.0 6.0 convolution_bitcast_fusion.1
  470.0 2.9 copy.24
  473.0 4.9 all-gather.4
  477.9 80.9 %all-gather.15.cloned.1.call-done = f32[32,128,1024]{2,1,0:T(8,128)} async-done(((f32[4,128,1024]{2,1,0:T(8,128)}), f32[32,128,1024]{2,1,0:T(8,128)}) %all-gather.15.cloned.1.call-update) | async-done | bytes 16777232 | tf_op jit(solution)/shard_map/all_gather | solution.py:31
  558.8 9.3 reduce_sum.37
  568.1 2.9 copy.49
  578.2 157.1 %all-reduce.9.cloned.1.call-done = f32[256,1024]{1,0:T(8,128)} async-done(((f32[256,1024]{1,0:T(8,128)}), f32[256,1024]{1,0:T(8,128)}) %all-reduce.9.cloned.1.call-update) | async-done | bytes 1048592 | tf_op jit(solution)/shard_map/psum | solution.py:21
  735.3 4.6 convolution_bitcast_fusion.2
  741.7 4.9 all-gather.6
  746.6 63.2 %all-gather.17.cloned.1.call-done = f32[24,128,1024]{2,1,0:T(8,128)} async-done(((f32[3,128,1024]{2,1,0:T(8,128)}), f32[24,128,1024]{2,1,0:T(8,128)}) %all-gather.17.cloned.1.call-update) | async-done | bytes 12582928 | tf_op jit(solution)/shard_map/all_gather | solution.py:31
  809.9 7.4 reduce_sum.38
  817.3 3.2 copy.50
  826.8 157.4 %all-reduce.11.cloned.1.call-done = f32[256,1024]{1,0:T(8,128)} async-done(((f32[256,1024]{1,0:T(8,128)}), f32[256,1024]{1,0:T(8,128)}) %all-reduce.11.cloned.1.call-update) | async-done | bytes 1048592 | tf_op jit(solution)/shard_map/psum | solution.py:21
  984.2 3.0 convolution_bitcast_fusion.3
  988.6 4.0 pad_maximum_fusion
  992.6 46.6 %all-gather.19.cloned.1.call-done = f32[16,128,1024]{2,1,0:T(8,128)} async-done(((f32[2,128,1024]{2,1,0:T(8,128)}), f32[16,128,1024]{2,1,0:T(8,128)}) %all-gather.19.cloned.1.call-update) | async-done | bytes 8388624 | tf_op jit(solution)/shard_map/all_gather | solution.py:31
  1039.2 4.4 reduce_sum.39
  (42 shorter events, 23.9 us)
Async XLA Ops:
  7.2 170.2 %all-reduce.5.cloned.1.call-start = ((), (), s32[]{:S(2)}) async-start(), calls=%async_computation | async-start | bytes 2097152 | tf_op jit(solution)/shard_map/psum | solution.py:21
  16.2 273.1 %all-gather.13.cloned.1.call-start = ((), (), s32[]{:S(2)}) async-start(), calls=%async_computation.4 | async-start | bytes 23592960 | tf_op jit(solution)/shard_map/all_gather | solution.py:31
  185.9 1.7 slice-start
  185.9 278.1 %all-reduce.7.cloned.1.call-start = ((), (), s32[]{:S(2)}) async-start(), calls=%async_computation.1 | async-start | bytes 2097152 | tf_op jit(solution)/shard_map/psum | solution.py:21
  304.6 254.2 %all-gather.15.cloned.1.call-start = ((), (), s32[]{:S(2)}) async-start(), calls=%async_computation.5 | async-start | bytes 18874368 | tf_op jit(solution)/shard_map/all_gather | solution.py:31
  472.9 262.4 %all-reduce.9.cloned.1.call-start = ((), (), s32[]{:S(2)}) async-start(), calls=%async_computation.2 | async-start | bytes 2097152 | tf_op jit(solution)/shard_map/psum | solution.py:21
  572.8 1.3 copy-start
  576.1 233.7 %all-gather.17.cloned.1.call-start = ((), (), s32[]{:S(2)}) async-start(), calls=%async_computation.6 | async-start | bytes 14155776 | tf_op jit(solution)/shard_map/all_gather | solution.py:31
  741.6 242.5 %all-reduce.11.cloned.1.call-start = ((), (), s32[]{:S(2)}) async-start(), calls=%async_computation.3 | async-start | bytes 2097152 | tf_op jit(solution)/shard_map/psum | solution.py:21
  817.3 3.2 copy-start.1
  822.0 1.2 copy-start.2
  825.2 213.9 %all-gather.19.cloned.1.call-start = ((), (), s32[]{:S(2)}) async-start(), calls=%async_computation.7 | async-start | bytes 9437184 | tf_op jit(solution)/shard_map/all_gather | solution.py:31
  826.8 161.8 %copy-start.4 = (f32[256,1024]{1,0:T(8,128)S(1)}, f32[256,1024]{1,0:T(8,128)}, u32[]{:S(2)}) copy-start(f32[256,1024]{1,0:T(8,128)} %all-reduce.7.cloned.1.call-done) | copy-start | bytes 3145732
  826.8 161.8 %copy-start.5 = (f32[256,1024]{1,0:T(8,128)S(1)}, f32[256,1024]{1,0:T(8,128)}, u32[]{:S(2)}) copy-start(f32[256,1024]{1,0:T(8,128)} %all-reduce.9.cloned.1.call-done) | copy-start | bytes 3145732
  1043.6 1.7 copy-start.3
Sparse Core Ops, SparseCore 0:
  16.4 161.0 all-reduce.4
  186.0 103.3 all-gather.12
  304.7 159.2 all-reduce.6
  473.0 85.6 all-gather.14
  576.3 159.0 all-reduce.8
  741.8 68.0 all-gather.16
  825.4 158.7 all-reduce.10
  988.7 50.4 all-gather.18
